TPU v7x, 32 devices: a whole 2x2x4 slice. The times are simulated.
32 devices in a mesh: row: 8 (over z, core), loop: 4 (over y, x).
Axes of the slice: x: 2, y: 2, z: 4, core: 2. Of those that a mesh axis runs over, the one named last changes fastest.
Arguments:
- student_image: bfloat16 [5120, 1024], P(('row', 'loop')), may hold values from -12 to 12
- student_text: bfloat16 [5120, 1024], P(('row', 'loop')), may hold values from -12 to 12
- teacher_image: bfloat16 [5120, 1024], P('row', 'loop'), may hold values from -12 to 12
- teacher_text: bfloat16 [5120, 1024], P('row', 'loop'), may hold values from -12 to 12
- student_scale: float32 [1], replicated, may hold values from 30 to 100
- teacher_scale: float32 [1], replicated, may hold values from 30 to 100
Outputs:
- loss: float32 [1], replicated
- grad_image: bfloat16 [5120, 1024], P(('row', 'loop'))
- grad_text: bfloat16 [5120, 1024], P(('row', 'loop'))
All inputs are finite; a program needn't handle non-finite values.
Results may differ from a plain program's by a relative error of at most 0.014.
The roundings to bfloat16 on the way count: a program that leaves them out, or rounds other values in their place, can miss the bound.
Values may be sent and summed in bfloat16 or wider, within the bound.
A program may use at most 128 MiB of HBM per device.

v0:
```python
import jax
import jax.numpy as jnp
from jax import lax
from jax.sharding import PartitionSpec as P

EPS = 1e-06


def unit_rows(codes):
    values = codes.astype(jnp.float32)
    norms = jnp.sqrt(jnp.sum(values * values, axis=1, keepdims=True) + EPS)
    return (values / norms, norms)


def back_norm(grad_unit, units, norms):
    inner = jnp.sum(grad_unit * units, axis=1, keepdims=True)
    return ((grad_unit - units * inner) / norms).astype(jnp.bfloat16)


def on_device(
    student_image, student_text, teacher_image, teacher_text, student_scale, teacher_scale
):
    simg_unit, simg_norm = unit_rows(student_image)
    stxt_unit, stxt_norm = unit_rows(student_text)
    simg_own = simg_unit.astype(jnp.bfloat16)
    stxt_own = stxt_unit.astype(jnp.bfloat16)
    timg_full = lax.all_gather(teacher_image, "loop", axis=1, tiled=True)
    timg = unit_rows(timg_full)[0].astype(jnp.bfloat16)
    ttxt_full = lax.all_to_all(teacher_text, "loop", split_axis=0, concat_axis=1, tiled=True)
    ttxt_own = unit_rows(ttxt_full)[0].astype(jnp.bfloat16)
    simg = lax.all_gather(simg_own, "loop", axis=0, tiled=True)
    stxt, ttxt = (
        lax.all_gather(stxt_own, "row", axis=0, tiled=True),
        lax.all_gather(ttxt_own, "row", axis=0, tiled=True),
    )
    sscale = student_scale[0]
    tscale = teacher_scale[0]
    slog = sscale * jnp.einsum("re,ce->rc", simg, stxt, preferred_element_type=jnp.float32)
    tlog = tscale * jnp.einsum("re,ce->rc", timg, ttxt, preferred_element_type=jnp.float32)
    smax, tmax = lax.pmax((jnp.max(slog, axis=1), jnp.max(tlog, axis=1)), "loop")
    sexp = jnp.exp(slog - smax[:, None])
    texp = jnp.exp(tlog - tmax[:, None])
    ssum, tsum, cross = lax.psum(
        (jnp.sum(sexp, axis=1), jnp.sum(texp, axis=1), jnp.sum(texp * (tlog - slog), axis=1)),
        "loop",
    )
    lses = smax + jnp.log(ssum)
    lset = tmax + jnp.log(tsum)
    diverge = cross / tsum - lset + lses
    group_total = lax.psum(jnp.sum(diverge), "row")
    batch_total = simg.shape[0] * lax.axis_size("row")
    loss = (group_total / batch_total).reshape(1)
    probs = jnp.exp(slog - lses[:, None])
    probt = jnp.exp(tlog - lset[:, None])
    grad_logits = (sscale * (probs - probt)).astype(jnp.bfloat16)
    dimg = lax.psum_scatter(
        jnp.dot(grad_logits, stxt, preferred_element_type=jnp.float32).astype(jnp.bfloat16),
        "loop",
        scatter_dimension=0,
        tiled=True,
    ).astype(jnp.float32)
    dtxt = lax.psum_scatter(
        jnp.einsum("rc,re->ce", grad_logits, simg, preferred_element_type=jnp.float32).astype(
            jnp.bfloat16
        ),
        "row",
        scatter_dimension=0,
        tiled=True,
    ).astype(jnp.float32)
    return (loss, back_norm(dimg, simg_unit, simg_norm), back_norm(dtxt, stxt_unit, stxt_norm))


def solution(mesh):
    return jax.shard_map(
        on_device,
        mesh=mesh,
        in_specs=(
            P(("row", "loop"), None),
            P(("row", "loop"), None),
            P("row", "loop"),
            P("row", "loop"),
            P(),
            P(),
        ),
        out_specs=(P(), P(("row", "loop"), None), P(("row", "loop"), None)),
        check_vma=False,
    )
```

profile of v0, /device:TPU:0, one launch (start us, length us, event | category | flops | bytes accessed | tf_op | source)
XLA Modules:
  0.0 265.1 jit_solution(4238910627074843657)
XLA Ops:
  9.1 1.8 fusion.14
  12.1 1.8 fusion.15
  14.0 14.7 %all_to_all.13 = bf16[4,160,256]{2,1,0:T(8,128)(2,1)S(1)} all-to-all(bf16[4,160,256]{2,1,0:T(8,128)(2,1)S(1)} %bitcast.19), channel_id=1, replica_groups=mesh['row'=8,'loop'=4] {'loop'}, dimensions={0} | all-to-all | bytes 655360 | tf_op jit(solution)/shard_map/all_to_all | solution.py:29
  31.2 12.3 %all-gather.5.cloned.1.call-done = bf16[640,1024]{1,0:T(8,128)(2,1)} async-done(((bf16[640,256]{1,0:T(8,128)(2,1)}), bf16[640,1024]{1,0:T(8,128)(2,1)}) %all-gather.5.cloned.1.call-update) | async-done | bytes 1310736 | tf_op jit(solution)/shard_map/all_gather | solution.py:27
  43.5 1.6 fusion.1
  45.2 29.5 %all-gather.9.cloned.1.call-done = bf16[640,1024]{1,0:T(8,128)(2,1)} async-done(((bf16[160,1024]{1,0:T(8,128)(2,1)}), bf16[640,1024]{1,0:T(8,128)(2,1)}) %all-gather.9.cloned.1.call-update) | async-done | bytes 1310736 | tf_op jit(solution)/shard_map/all_gather | solution.py:31
  74.6 35.4 %all-gather.11.cloned.1.call-done = bf16[1280,1024]{1,0:T(8,128)(2,1)} async-done(((bf16[160,1024]{1,0:T(8,128)(2,1)}), bf16[1280,1024]{1,0:T(8,128)(2,1)}) %all-gather.11.cloned.1.call-update) | async-done | bytes 2621456 | tf_op jit(solution)/shard_map/all_gather | solution.py:33
  110.0 4.2 %fusion.16 = (f32[640]{0:T(1024)S(1)}, f32[640,1280]{1,0:T(8,128)S(1)}) fusion(bf16[640,1024]{1,0:T(8,128)(2,1)} %all-gather.9.cloned.1.call-done, bf16[1280,1024]{1,0:T(8,128)(2,1)} %all-gather.11.cloned.1.call-done, f32[]{:T(128)} %bitcast.15), kind=kOutput, calls=%fused_computation.43 | convolution fusion | flops 1679359360 | bytes 7211524 | tf_op jit(solution)/shard_map/re,ce->rc/dot_general | solution.py:38
  114.2 30.8 %all-gather.7.cloned.1.call-done = bf16[1280,1024]{1,0:T(8,128)(2,1)} async-done(((bf16[160,1024]{1,0:T(8,128)(2,1)}), bf16[1280,1024]{1,0:T(8,128)(2,1)}) %all-gather.7.cloned.1.call-update) | async-done | bytes 2621456 | tf_op jit(solution)/shard_map/all_gather | solution.py:34
  144.9 5.8 %fusion.17 = (f32[640]{0:T(1024)S(1)}, f32[640,1280]{1,0:T(8,128)}) fusion(bf16[1280,1024]{1,0:T(8,128)(2,1)} %all-gather.7.cloned.1.call-done, bf16[640,1024]{1,0:T(8,128)(2,1)} %all-gather.5.cloned.1.call-done, f32[640]{0:T(1024)S(1)} %add_sqrt_fusion, f32[]{:T(128)} %bitcast.17), kind=kOutput, calls=%fused_computation.44 | convolution fusion | flops 1681325440 | bytes 7214084 | tf_op jit(solution)/shard_map/re,ce->rc/dot_general | solution.py:39
  150.7 10.0 %all-reduce.1 = (f32[640]{0:T(1024)S(1)}, f32[640]{0:T(1024)S(1)}) all-reduce(f32[640]{0:T(1024)S(1)} %get-tuple-element.14, f32[640]{0:T(1024)S(1)} %get-tuple-element.16), channel_id=1, replica_groups=mesh['row'=8,'loop'=4] {'loop'}, use_global_device_ids=true, to_apply=%region_11.0 | all-reduce | flops 1280 | bytes 10240 | tf_op jit(solution)/shard_map/pmax | solution.py:40
  160.7 3.3 %multiply_reduce_fusion = (f32[640]{0:T(1024)S(1)}, f32[640]{0:T(1024)S(1)}, f32[640]{0:T(1024)S(1)}) fusion(f32[640,1280]{1,0:T(8,128)} %get-tuple-element.17, f32[640,1280]{1,0:T(8,128)S(1)} %get-tuple-element.15, f32[640]{0:T(1024)S(1)} %get-tuple-element.10, f32[640]{0:T(1024)S(1)} %get-tuple-element.9), kind=kLoop, calls=%fused_computation.5 | loop fusion | flops 5732480 | bytes 6566400 | tf_op jit(solution)/shard_map/reduce_sum | solution.py:44
  164.0 14.0 %all-reduce = (f32[640]{0:T(1024)S(1)}, f32[640]{0:T(1024)S(1)}, f32[640]{0:T(1024)S(1)}) all-reduce(f32[640]{0:T(1024)S(1)} %get-tuple-element.5, f32[640]{0:T(1024)S(1)} %get-tuple-element.4, f32[640]{0:T(1024)S(1)} %get-tuple-element.3), channel_id=1, replica_groups=mesh['row'=8,'loop'=4] {'loop'}, use_global_device_ids=true, to_apply=%region_13.0 | all-reduce | flops 1920 | bytes 15360 | tf_op jit(solution)/shard_map/psum | solution.py:43
  178.7 3.0 %multiply_convert_fusion = bf16[640,1280]{1,0:T(8,128)(2,1)S(1)} fusion(f32[640,1280]{1,0:T(8,128)} %get-tuple-element.17, f32[640,1280]{1,0:T(8,128)S(1)} %get-tuple-element.15, f32[640]{0:T(1024)S(1)} %get-tuple-element.12, f32[640]{0:T(1024)S(1)} %get-tuple-element.13, f32[]{:T(128)} %bitcast.16), kind=kLoop, calls=%fused_computation.3 | loop fusion | flops 4096000 | bytes 8197124 | tf_op jit(solution)/shard_map/convert_element_type | solution.py:55
  181.7 1.2 copy-done.2
  182.9 3.0 %convolution_convert_fusion.1 = bf16[640,1024]{1,0:T(8,128)(2,1)} fusion(bf16[640,1280]{1,0:T(8,128)(2,1)S(1)} %multiply_convert_fusion, bf16[1280,1024]{1,0:T(8,128)(2,1)S(1)} %copy-done.4), kind=kOutput, calls=%fused_computation.12 | convolution fusion | flops 1678376960 | bytes 5570560 | tf_op jit(solution)/shard_map/dot_general | solution.py:57
  186.0 5.2 %convolution_convert_fusion = bf16[1280,1024]{1,0:T(8,128)(2,1)} fusion(bf16[640,1280]{1,0:T(8,128)(2,1)} %copy-done.2, bf16[640,1024]{1,0:T(8,128)(2,1)S(1)} %copy-done.5), kind=kOutput, calls=%fused_computation | convolution fusion | flops 1679032320 | bytes 5570560 | tf_op jit(solution)/shard_map/rc,re->ce/dot_general | solution.py:63
  191.2 14.2 %psum.31 = f32[]{:T(128)} all-reduce(f32[]{:T(128)} %get-tuple-element.11), channel_id=1, replica_groups=mesh['row'=8,'loop'=4] {'row'}, use_global_device_ids=true, to_apply=%region_15.0 | all-reduce | flops 1 | bytes 8 | tf_op jit(solution)/shard_map/psum | solution.py:50
  206.1 7.7 %reduce-scatter.3.cloned.1.call-done = bf16[160,1024]{1,0:T(8,128)(2,1)} async-done(((bf16[640,1024]{1,0:T(8,128)(2,1)}), bf16[160,1024]{1,0:T(8,128)(2,1)}) %reduce-scatter.3.cloned.1.call-update) | async-done | bytes 327696 | tf_op jit(solution)/shard_map/reduce_scatter | solution.py:56
  213.8 1.2 fusion.7
  215.0 2.0 fusion.9
  217.0 37.0 %reduce-scatter.5.cloned.1.call-done = bf16[160,1024]{1,0:T(8,128)(2,1)} async-done(((bf16[1280,1024]{1,0:T(8,128)(2,1)}), bf16[160,1024]{1,0:T(8,128)(2,1)}) %reduce-scatter.5.cloned.1.call-update) | async-done | bytes 327696 | tf_op jit(solution)/shard_map/reduce_scatter | solution.py:62
  253.9 1.2 fusion.10
  255.2 2.0 fusion.12
  (34 shorter events, 5.0 us)
Async XLA Ops:
  7.2 6.9 %copy-start.3 = (bf16[640,256]{1,0:T(8,128)(2,1)S(1)}, bf16[640,256]{1,0:T(8,128)(2,1)}, u32[]{:S(2)}) copy-start(bf16[640,256]{1,0:T(8,128)(2,1)} %param.9) | copy-start | bytes 983044
  7.2 36.3 %all-gather.5.cloned.1.call-start = ((), (), s32[]{:S(2)}) async-start(), calls=%async_computation.3 | async-start | bytes 1638400 | tf_op jit(solution)/shard_map/all_gather | solution.py:27
  7.9 66.7 %all-gather.9.cloned.1.call-start = ((), (), s32[]{:S(2)}) async-start(), calls=%async_computation.5 | async-start | bytes 1638400 | tf_op jit(solution)/shard_map/all_gather | solution.py:31
  10.9 99.1 %all-gather.11.cloned.1.call-start = ((), (), s32[]{:S(2)}) async-start(), calls=%async_computation.6 | async-start | bytes 2949120 | tf_op jit(solution)/shard_map/all_gather | solution.py:33
  14.0 131.0 %all-gather.7.cloned.1.call-start = ((), (), s32[]{:S(2)}) async-start(), calls=%async_computation.4 | async-start | bytes 2949120 | tf_op jit(solution)/shard_map/all_gather | solution.py:34
  29.9 183.9 %reduce-scatter.3.cloned.1.call-start = ((), (), s32[]{:S(2)}) async-start(), calls=%async_computation.7 | async-start | bytes 1638400 | tf_op jit(solution)/shard_map/reduce_scatter | solution.py:56
  178.7 4.2 %copy-start.4 = (bf16[1280,1024]{1,0:T(8,128)(2,1)S(1)}, bf16[1280,1024]{1,0:T(8,128)(2,1)}, u32[]{:S(2)}) copy-start(bf16[1280,1024]{1,0:T(8,128)(2,1)} %all-gather.11.cloned.1.call-done) | copy-start | bytes 7864324
  181.7 1.2 copy-start.2
  182.9 3.1 %copy-start.5 = (bf16[640,1024]{1,0:T(8,128)(2,1)S(1)}, bf16[640,1024]{1,0:T(8,128)(2,1)}, u32[]{:S(2)}) copy-start(bf16[640,1024]{1,0:T(8,128)(2,1)} %all-gather.9.cloned.1.call-done) | copy-start | bytes 3932164
  185.9 68.0 %reduce-scatter.5.cloned.1.call-start = ((), (), s32[]{:S(2)}) async-start(), calls=%async_computation.8 | async-start | bytes 2949120 | tf_op jit(solution)/shard_map/reduce_scatter | solution.py:62
  191.2 22.6 %copy-start = (bf16[160,1024]{1,0:T(8,128)(2,1)S(1)}, bf16[160,1024]{1,0:T(8,128)(2,1)}, u32[]{:S(2)}) copy-start(bf16[160,1024]{1,0:T(8,128)(2,1)} %param.6) | copy-start | bytes 983044
  191.2 62.8 %copy-start.1 = (bf16[160,1024]{1,0:T(8,128)(2,1)S(1)}, bf16[160,1024]{1,0:T(8,128)(2,1)}, u32[]{:S(2)}) copy-start(bf16[160,1024]{1,0:T(8,128)(2,1)} %param.7) | copy-start | bytes 983044
Sparse Core Ops, SparseCore 0:
  9.8 33.6 all-gather.4
  45.9 28.6 all-gather.8
  76.3 33.6 all-gather.10
  112.1 32.8 all-gather.6
  186.0 27.6 reduce-scatter.2
  215.9 37.9 reduce-scatter.4
where the time goes:
time: 266 us; the launch traced here: 265 us
  waiting for transfers between devices  153 us (58%)
  blocking collectives  52.9 us (20%)
  other arithmetic  22 us (8%)
  matrix products  18.1 us (7%)
  between operations  17.3 us (7%)
    reduce_scatter x1, waiting for transfers between devices, on_device(): lax.psum_scatter(jnp.einsum('rc,re->ce', grad_logits, simg, preferred_ele...  37 us
    all_gather x1, waiting for transfers between devices, on_device(): lax.all_gather(stxt_own, 'row', axis=0, tiled=True)  35.4 us
    all_gather x1, waiting for transfers between devices, on_device(): lax.all_gather(ttxt_own, 'row', axis=0, tiled=True)  30.8 us
    all_gather x1, waiting for transfers between devices, on_device(): simg = lax.all_gather(simg_own, 'loop', axis=0, tiled=True)  29.5 us
    all_to_all x1, blocking collectives, on_device(): lax.all_to_all(teacher_text, 'loop', split_axis=0, concat_axis=1, tiled=T...  14.7 us
    psum x1, blocking collectives, on_device(): group_total = lax.psum(jnp.sum(diverge), 'row')  14.2 us
    psum x1, blocking collectives, on_device(): lax.psum((jnp.sum(sexp, axis=1), jnp.sum(texp, axis=1), jnp.sum(texp * (t...  14 us
    all_gather x1, waiting for transfers between devices, on_device(): timg_full = lax.all_gather(teacher_image, 'loop', axis=1, tiled=True)  12.3 us
  transfers between devices with their start and end apart: 6, of which 6 were waited for; matrix products, arithmetic and copies ran while one was open for 8% of the time, Pallas kernels for 0%

commit v1 on v0

--- a/solution.py
+++ b/solution.py
@@ -31,7 +31,9 @@
     simg = lax.all_gather(simg_own, "loop", axis=0, tiled=True)
     stxt, ttxt = (
         lax.all_gather(stxt_own, "row", axis=0, tiled=True),
-        lax.all_gather(ttxt_own, "row", axis=0, tiled=True),
+        jnp.concatenate(
+            lax.all_to_all(jnp.stack([ttxt_own] * lax.axis_size("row")), "row", 0, 0), axis=0
+        ),
     )
     sscale = student_scale[0]
     tscale = teacher_scale[0]

time: 266 us -> 236 us (0.89)
  waiting for transfers between devices: 153 us -> 128 us
  blocking collectives: 52.9 us -> 38.2 us
  starting transfers between devices: 0.24 us -> 10.2 us
    all_gather x1 -> x0, waiting for transfers between devices: 30.8 us -> none  [on_device(): lax.all_gather(ttxt_own, 'row', axis=0, tiled=True)]
    all_to_all x1 -> x0, blocking collectives: 14.7 us -> none  [on_device(): lax.all_to_all(teacher_text, 'loop', split_axis=0, concat_axis=1, tiled=T...]
    all_to_all x0 -> x2, starting transfers between devices: none -> 10.1 us  [the longest x1 5.2 us: on_device(): lax.all_to_all(teacher_text, 'loop', split_axis=0, concat_axis=1, tiled=T...]
    all_gather x1, waiting for transfers between devices: 35.4 us -> 39.9 us  [on_device(): lax.all_gather(stxt_own, 'row', axis=0, tiled=True)]
    all_to_all x0 -> x2, waiting for transfers between devices: none -> 3.87 us  [the longest x1 3.86 us: on_device(): lax.all_to_all(teacher_text, 'loop', split_axis=0, concat_axis=1, tiled=T...]
  transfers between devices with their start and end apart: 6 -> 7, of which waited for: 6 -> 6; matrix products, arithmetic and copies ran while one was open for 8% -> 9% of each run, Pallas kernels for 0% -> 0%
where the time goes in v1:
time: 236 us; the launch traced here: 235 us
  waiting for transfers between devices  128 us (54%)
  blocking collectives  38.2 us (16%)
  other arithmetic  20.3 us (9%)
  matrix products  18.1 us (8%)
  between operations  17 us (7%)
  starting transfers between devices  10.2 us (4%)
  local copies, waits for them, and re-layouts  3.11 us (1%)
    all_gather x1, waiting for transfers between devices, on_device(): lax.all_gather(stxt_own, 'row', axis=0, tiled=True)  39.9 us
    reduce_scatter x1, waiting for transfers between devices, on_device(): lax.psum_scatter(jnp.einsum('rc,re->ce', grad_logits, simg, preferred_ele...  36.8 us
    all_gather x1, waiting for transfers between devices, on_device(): simg = lax.all_gather(simg_own, 'loop', axis=0, tiled=True)  29.5 us
    psum x1, blocking collectives, on_device(): lax.psum((jnp.sum(sexp, axis=1), jnp.sum(texp, axis=1), jnp.sum(texp * (t...  14.9 us
    psum x1, blocking collectives, on_device(): group_total = lax.psum(jnp.sum(diverge), 'row')  14.2 us
    all_gather x1, waiting for transfers between devices, on_device(): timg_full = lax.all_gather(teacher_image, 'loop', axis=1, tiled=True)  10.6 us
    pmax x1, blocking collectives, on_device(): lax.pmax((jnp.max(slog, axis=1), jnp.max(tlog, axis=1)), 'loop')  9.03 us
    reduce_scatter x1, waiting for transfers between devices, on_device(): lax.psum_scatter(jnp.dot(grad_logits, stxt, preferred_element_type=jnp.fl...  6.64 us
  transfers between devices with their start and end apart: 7, of which 6 were waited for; matrix products, arithmetic and copies ran while one was open for 9% of the time, Pallas kernels for 0%

profile of v1, /device:TPU:0, one launch (start us, length us, event | category | flops | bytes accessed | tf_op | source)
XLA Modules:
  0.0 234.9 jit_solution(9843186742077251693)
XLA Ops:
  9.1 1.8 fusion.14
  10.9 5.2 %all-to-all-start = ((bf16[4,160,256]{2,1,0:T(8,128)(2,1)}), bf16[4,160,256]{2,1,0:T(8,128)(2,1)S(1)}, u32[]{:S(2)}, u32[]{:S(2)}) async-start(bf16[4,160,256]{2,1,0:T(8,128)(2,1)} %bitcast.20), calls=%async_computation | async-start | bytes 655360 | tf_op jit(solution)/shard_map/all_to_all | solution.py:29
  18.2 3.9 %all-to-all-done = bf16[4,160,256]{2,1,0:T(8,128)(2,1)S(1)} async-done(((bf16[4,160,256]{2,1,0:T(8,128)(2,1)}), bf16[4,160,256]{2,1,0:T(8,128)(2,1)S(1)}, u32[]{:S(2)}, u32[]{:S(2)}) %all-to-all-start) | async-done | bytes 327712 | tf_op jit(solution)/shard_map/all_to_all | solution.py:29
  22.5 1.8 stack.2
  24.3 4.9 %all-to-all-start.1 = ((bf16[8,160,1024]{2,1,0:T(8,128)(2,1)}), bf16[8,160,1024]{2,1,0:T(8,128)(2,1)}, u32[]{:S(2)}, u32[]{:S(2)}) async-start(bf16[8,160,1024]{2,1,0:T(8,128)(2,1)} %stack.2), calls=%async_computation.1 | async-start | bytes 5242880 | tf_op jit(solution)/shard_map/all_to_all | solution.py:35
  30.5 10.6 %all-gather.4.cloned.1.call-done = bf16[640,1024]{1,0:T(8,128)(2,1)} async-done(((bf16[640,256]{1,0:T(8,128)(2,1)}), bf16[640,1024]{1,0:T(8,128)(2,1)}) %all-gather.4.cloned.1.call-update) | async-done | bytes 1310736 | tf_op jit(solution)/shard_map/all_gather | solution.py:27
  41.1 1.6 fusion.1
  42.8 29.5 %all-gather.6.cloned.1.call-done = bf16[640,1024]{1,0:T(8,128)(2,1)} async-done(((bf16[160,1024]{1,0:T(8,128)(2,1)}), bf16[640,1024]{1,0:T(8,128)(2,1)}) %all-gather.6.cloned.1.call-update) | async-done | bytes 1310736 | tf_op jit(solution)/shard_map/all_gather | solution.py:31
  72.2 39.9 %all-gather.8.cloned.1.call-done = bf16[1280,1024]{1,0:T(8,128)(2,1)} async-done(((bf16[160,1024]{1,0:T(8,128)(2,1)}), bf16[1280,1024]{1,0:T(8,128)(2,1)}) %all-gather.8.cloned.1.call-update) | async-done | bytes 2621456 | tf_op jit(solution)/shard_map/all_gather | solution.py:33
  112.1 4.2 %fusion.16 = (f32[640]{0:T(1024)S(1)}, f32[640,1280]{1,0:T(8,128)S(1)}) fusion(bf16[640,1024]{1,0:T(8,128)(2,1)} %all-gather.6.cloned.1.call-done, bf16[1280,1024]{1,0:T(8,128)(2,1)} %all-gather.8.cloned.1.call-done, f32[]{:T(128)} %bitcast.16), kind=kOutput, calls=%fused_computation.43 | convolution fusion | flops 1679359360 | bytes 7211524 | tf_op jit(solution)/shard_map/re,ce->rc/dot_general | solution.py:40
  116.3 5.8 %fusion.17 = (f32[640]{0:T(1024)S(1)}, f32[640,1280]{1,0:T(8,128)}) fusion(bf16[1280,1024]{1,0:T(8,128)(2,1)} %bitcast.3, bf16[640,1024]{1,0:T(8,128)(2,1)} %all-gather.4.cloned.1.call-done, f32[640]{0:T(1024)S(1)} %add_sqrt_fusion, f32[]{:T(128)} %bitcast.18), kind=kOutput, calls=%fused_computation.44 | convolution fusion | flops 1681325440 | bytes 7214084 | tf_op jit(solution)/shard_map/re,ce->rc/dot_general | solution.py:41
  122.1 9.0 %all-reduce.1 = (f32[640]{0:T(1024)S(1)}, f32[640]{0:T(1024)S(1)}) all-reduce(f32[640]{0:T(1024)S(1)} %get-tuple-element.14, f32[640]{0:T(1024)S(1)} %get-tuple-element.16), channel_id=1, replica_groups=mesh['row'=8,'loop'=4] {'loop'}, use_global_device_ids=true, to_apply=%region_11.0 | all-reduce | flops 1280 | bytes 10240 | tf_op jit(solution)/shard_map/pmax | solution.py:42
  131.1 3.3 %multiply_reduce_fusion = (f32[640]{0:T(1024)S(1)}, f32[640]{0:T(1024)S(1)}, f32[640]{0:T(1024)S(1)}) fusion(f32[640,1280]{1,0:T(8,128)} %get-tuple-element.17, f32[640,1280]{1,0:T(8,128)S(1)} %get-tuple-element.15, f32[640]{0:T(1024)S(1)} %get-tuple-element.10, f32[640]{0:T(1024)S(1)} %get-tuple-element.9), kind=kLoop, calls=%fused_computation.5 | loop fusion | flops 5732480 | bytes 6566400 | tf_op jit(solution)/shard_map/reduce_sum | solution.py:46
  134.4 14.9 %all-reduce = (f32[640]{0:T(1024)S(1)}, f32[640]{0:T(1024)S(1)}, f32[640]{0:T(1024)S(1)}) all-reduce(f32[640]{0:T(1024)S(1)} %get-tuple-element.5, f32[640]{0:T(1024)S(1)} %get-tuple-element.4, f32[640]{0:T(1024)S(1)} %get-tuple-element.3), channel_id=1, replica_groups=mesh['row'=8,'loop'=4] {'loop'}, use_global_device_ids=true, to_apply=%region_13.0 | all-reduce | flops 1920 | bytes 15360 | tf_op jit(solution)/shard_map/psum | solution.py:45
  150.0 3.0 %multiply_convert_fusion = bf16[640,1280]{1,0:T(8,128)(2,1)S(1)} fusion(f32[640,1280]{1,0:T(8,128)} %get-tuple-element.17, f32[640,1280]{1,0:T(8,128)S(1)} %get-tuple-element.15, f32[640]{0:T(1024)S(1)} %get-tuple-element.12, f32[640]{0:T(1024)S(1)} %get-tuple-element.13, f32[]{:T(128)} %bitcast.17), kind=kLoop, calls=%fused_computation.3 | loop fusion | flops 4096000 | bytes 8197124 | tf_op jit(solution)/shard_map/convert_element_type | solution.py:57
  154.2 3.0 %convolution_convert_fusion.1 = bf16[640,1024]{1,0:T(8,128)(2,1)} fusion(bf16[640,1280]{1,0:T(8,128)(2,1)S(1)} %multiply_convert_fusion, bf16[1280,1024]{1,0:T(8,128)(2,1)S(1)} %copy-done.4), kind=kOutput, calls=%fused_computation.12 | convolution fusion | flops 1678376960 | bytes 5570560 | tf_op jit(solution)/shard_map/dot_general | solution.py:59
  157.3 5.2 %convolution_convert_fusion = bf16[1280,1024]{1,0:T(8,128)(2,1)} fusion(bf16[640,1280]{1,0:T(8,128)(2,1)} %copy-done.3, bf16[640,1024]{1,0:T(8,128)(2,1)S(1)} %copy-done.5), kind=kOutput, calls=%fused_computation | convolution fusion | flops 1679032320 | bytes 5570560 | tf_op jit(solution)/shard_map/rc,re->ce/dot_general | solution.py:65
  162.5 14.2 %psum.31 = f32[]{:T(128)} all-reduce(f32[]{:T(128)} %get-tuple-element.11), channel_id=1, replica_groups=mesh['row'=8,'loop'=4] {'row'}, use_global_device_ids=true, to_apply=%region_15.0 | all-reduce | flops 1 | bytes 8 | tf_op jit(solution)/shard_map/psum | solution.py:52
  177.4 6.6 %reduce-scatter.3.cloned.1.call-done = bf16[160,1024]{1,0:T(8,128)(2,1)} async-done(((bf16[640,1024]{1,0:T(8,128)(2,1)}), bf16[160,1024]{1,0:T(8,128)(2,1)}) %reduce-scatter.3.cloned.1.call-update) | async-done | bytes 327696 | tf_op jit(solution)/shard_map/reduce_scatter | solution.py:58
  184.0 1.2 fusion.7
  185.3 2.0 fusion.9
  187.2 36.8 %reduce-scatter.5.cloned.1.call-done = bf16[160,1024]{1,0:T(8,128)(2,1)} async-done(((bf16[1280,1024]{1,0:T(8,128)(2,1)}), bf16[160,1024]{1,0:T(8,128)(2,1)}) %reduce-scatter.5.cloned.1.call-update) | async-done | bytes 327696 | tf_op jit(solution)/shard_map/reduce_scatter | solution.py:64
  224.0 1.2 fusion.10
  225.3 2.0 fusion.12
  (35 shorter events, 6.2 us)
Async XLA Ops:
  7.2 10.1 %copy-start.1 = (bf16[160,1024]{1,0:T(8,128)(2,1)S(1)}, bf16[160,1024]{1,0:T(8,128)(2,1)}, u32[]{:S(2)}) copy-start(bf16[160,1024]{1,0:T(8,128)(2,1)} %param.7) | copy-start | bytes 983044
  7.2 33.9 %all-gather.4.cloned.1.call-start = ((), (), s32[]{:S(2)}) async-start(), calls=%async_computation.4 | async-start | bytes 1638400 | tf_op jit(solution)/shard_map/all_gather | solution.py:27
  7.9 64.3 %all-gather.6.cloned.1.call-start = ((), (), s32[]{:S(2)}) async-start(), calls=%async_computation.5 | async-start | bytes 1638400 | tf_op jit(solution)/shard_map/all_gather | solution.py:31
  10.9 11.1 %all-to-all-start = ((bf16[4,160,256]{2,1,0:T(8,128)(2,1)}), bf16[4,160,256]{2,1,0:T(8,128)(2,1)S(1)}, u32[]{:S(2)}, u32[]{:S(2)}) async-start(bf16[4,160,256]{2,1,0:T(8,128)(2,1)} %bitcast.20), calls=%async_computation | async-start | bytes 655360 | tf_op jit(solution)/shard_map/all_to_all | solution.py:29
  16.2 96.0 %all-gather.8.cloned.1.call-start = ((), (), s32[]{:S(2)}) async-start(), calls=%async_computation.6 | async-start | bytes 2949120 | tf_op jit(solution)/shard_map/all_gather | solution.py:33
  24.3 92.0 %all-to-all-start.1 = ((bf16[8,160,1024]{2,1,0:T(8,128)(2,1)}), bf16[8,160,1024]{2,1,0:T(8,128)(2,1)}, u32[]{:S(2)}, u32[]{:S(2)}) async-start(bf16[8,160,1024]{2,1,0:T(8,128)(2,1)} %stack.2), calls=%async_computation.1 | async-start | bytes 5242880 | tf_op jit(solution)/shard_map/all_to_all | solution.py:35
  29.2 154.9 %reduce-scatter.3.cloned.1.call-start = ((), (), s32[]{:S(2)}) async-start(), calls=%async_computation.7 | async-start | bytes 1638400 | tf_op jit(solution)/shard_map/reduce_scatter | solution.py:58
  150.0 4.2 %copy-start.4 = (bf16[1280,1024]{1,0:T(8,128)(2,1)S(1)}, bf16[1280,1024]{1,0:T(8,128)(2,1)}, u32[]{:S(2)}) copy-start(bf16[1280,1024]{1,0:T(8,128)(2,1)} %all-gather.8.cloned.1.call-done) | copy-start | bytes 7864324
  153.0 1.2 copy-start.3
  154.2 3.1 %copy-start.5 = (bf16[640,1024]{1,0:T(8,128)(2,1)S(1)}, bf16[640,1024]{1,0:T(8,128)(2,1)}, u32[]{:S(2)}) copy-start(bf16[640,1024]{1,0:T(8,128)(2,1)} %all-gather.6.cloned.1.call-done) | copy-start | bytes 3932164
  157.2 66.8 %reduce-scatter.5.cloned.1.call-start = ((), (), s32[]{:S(2)}) async-start(), calls=%async_computation.8 | async-start | bytes 2949120 | tf_op jit(solution)/shard_map/reduce_scatter | solution.py:64
  162.5 21.6 %copy-start = (bf16[160,1024]{1,0:T(8,128)(2,1)S(1)}, bf16[160,1024]{1,0:T(8,128)(2,1)}, u32[]{:S(2)}) copy-start(bf16[160,1024]{1,0:T(8,128)(2,1)} %param.6) | copy-start | bytes 983044
  162.5 61.6 %copy-start.2 = (bf16[160,1024]{1,0:T(8,128)(2,1)S(1)}, bf16[160,1024]{1,0:T(8,128)(2,1)}, u32[]{:S(2)}) copy-start(bf16[160,1024]{1,0:T(8,128)(2,1)} %param.7) | copy-start | bytes 983044
Sparse Core Ops, SparseCore 0:
  9.8 31.2 all-gather.3
  43.5 28.6 all-gather.5
  74.4 37.6 all-gather.7
  157.3 26.6 reduce-scatter.2
  186.2 37.8 reduce-scatter.4
